TPU v7x, 512 devices: a whole 4x4x16 slice. The times are simulated.
512 devices in a mesh: grp: 16 (over z_lo, core), seq: 32 (over x, z_hi, y).
Axes of the slice: x: 4, y: 4, z: 16 (z_hi: 2, z_lo: 8; z = z_hi * 8 + z_lo), core: 2. Of those that a mesh axis runs over, the one named last changes fastest.
Arguments:
- queries: bfloat16 [65536, 3072], P(('grp', 'seq')), may hold values from -6 to 6, as said below
- key_states: bfloat16 [65536, 3072], P(('grp', 'seq')), may hold values from -6 to 6
- value_states: bfloat16 [65536, 3072], P(('grp', 'seq')), may hold values from -16 to 16
- key_keep: int32 [65536], P(('grp', 'seq')), may hold values 0 or 1
- summary_pos: int32 [16], replicated, may hold values from 0 to 31
Outputs:
- attended: bfloat16 [65536, 3072], P(('grp', 'seq'))
Inputs may be any that keep to these rules, and one draw needn't show every extreme that they name: queries and key_states entries lie within -6 to 6.
All inputs are finite; a program needn't handle non-finite values. No bound on the sum of `key_keep` on one device may be relied on, other than what follows from the above.
Results may differ from a plain program's by a relative error of at most 0.008.
Values may be sent and summed in bfloat16 or wider, within the bound.
No kernel may reach another device: no remote copies, remote signals or barrier semaphores. Data moves between devices by JAX's collectives and lax.ppermute only.
A program may use at most 64 MiB of HBM per device.

v0:
```python
import math
import jax
import jax.numpy as jnp
from jax import lax
from jax.sharding import PartitionSpec as P

HEADS = 24
HEAD_DIM = 128
FIXED_HEADS = 4
STRIDED_HEADS = 4
LOCAL_HEADS = 16
BLOCK = 128
LOOKBACK = 2
NEG = -1e30


def passed_along(block, axis, distance):
    devices = range(lax.axis_size(axis))
    route = [(i - distance, i) for i in devices if i - distance in devices]
    return lax.ppermute(block, axis, route)


def spread(value, axis, source):
    kept = jnp.where(lax.axis_index(axis) == source, value, 0).astype(value.dtype)
    return lax.psum(kept, axis)


def partial_softmax(query_heads, key_rows, value_rows, allowed):
    scores = jnp.einsum(
        "qhd,khd->hqk", query_heads, key_rows, preferred_element_type=jnp.float32
    ) / math.sqrt(HEAD_DIM)
    scores = jnp.where(allowed[None], scores, NEG)
    row_max = jnp.max(scores, axis=2)
    weights = jnp.where(allowed[None], jnp.exp(scores - row_max[:, :, None]), 0.0)
    row_sum = jnp.sum(weights, axis=2)
    weighted = jnp.einsum(
        "hqk,khd->hqd", weights.astype(jnp.bfloat16), value_rows, preferred_element_type=jnp.float32
    )
    return (row_max, row_sum, weighted)


def merge_state(left_part, right_part):
    row_max = jnp.maximum(left_part[0], right_part[0])
    left_scale = jnp.exp(left_part[0] - row_max)
    right_scale = jnp.exp(right_part[0] - row_max)
    row_sum = left_part[1] * left_scale + right_part[1] * right_scale
    weighted = left_part[2] * left_scale[:, :, None] + right_part[2] * right_scale[:, :, None]
    return (row_max, row_sum, weighted)


def blank_state(count):
    return (
        jnp.full((count, BLOCK), NEG, jnp.float32),
        jnp.zeros((count, BLOCK), jnp.float32),
        jnp.zeros((count, BLOCK, HEAD_DIM), jnp.float32),
    )


def head_range(state, head_lo, head_hi):
    return tuple((member[head_lo:head_hi] for member in state))


def on_device(queries, key_states, value_states, key_keep, summary_pos):
    stride = lax.axis_size("seq")
    groups = lax.axis_size("grp")
    column = lax.axis_index("seq")
    window = lax.axis_index("grp")
    block_id = window * stride + column
    lane_ids = jnp.arange(BLOCK, dtype=jnp.int32)
    group_ids = jnp.arange(groups, dtype=jnp.int32)
    query_heads = queries.reshape(BLOCK, HEADS, HEAD_DIM)
    keep_flag = key_keep.astype(jnp.bfloat16)
    own_block = (key_states, value_states, keep_flag)

    def all_heads(block_rows, allowed):
        return partial_softmax(
            query_heads,
            block_rows[0].reshape(BLOCK, HEADS, HEAD_DIM),
            block_rows[1].reshape(BLOCK, HEADS, HEAD_DIM),
            allowed,
        )

    diagonal = lane_ids[:, None] == lane_ids[None, :]
    causal = (lane_ids[None, :] <= lane_ids[:, None]) & ((key_keep[None, :] == 1) | diagonal)
    near_state = all_heads(own_block, causal)
    prior_one = passed_along((own_block[0], own_block[1], own_block[2]), ("grp", "seq"), 1)
    prior_two = passed_along((own_block[0], own_block[1], own_block[2]), ("grp", "seq"), 2)
    for earlier in (prior_one, prior_two):
        allowed = jnp.broadcast_to((earlier[2] > 0)[None, :], (BLOCK, BLOCK))
        near_state = merge_state(near_state, all_heads(earlier, allowed))
    fixed_lo = LOCAL_HEADS * HEAD_DIM
    fixed_hi = (LOCAL_HEADS + FIXED_HEADS) * HEAD_DIM
    root_dev = summary_pos[window]
    summary_own = (key_states[:, fixed_lo:fixed_hi], value_states[:, fixed_lo:fixed_hi], keep_flag)
    summary_here = (
        spread(summary_own[0], "seq", root_dev),
        spread(summary_own[1], "seq", root_dev),
        spread(summary_own[2], "seq", root_dev),
    )
    fixed_queries = query_heads[:, LOCAL_HEADS : LOCAL_HEADS + FIXED_HEADS]
    shard_rows = (
        lax.all_gather(summary_here[0], "grp", axis=0, tiled=True),
        lax.all_gather(summary_here[1], "grp", axis=0, tiled=True),
        lax.all_gather(summary_here[2], "grp", axis=0, tiled=True),
    )
    row_count = shard_rows[0].shape[0]
    row_window = jnp.arange(row_count, dtype=jnp.int32) // BLOCK
    hit_mask = row_window[:, None] == group_ids[None, :]
    row_summary = jnp.sum(jnp.where(hit_mask, summary_pos[None, :], 0), axis=1)
    usable = (row_window * stride + row_summary < block_id - LOOKBACK) & (shard_rows[2] > 0)
    allowed = jnp.broadcast_to(usable[None, :], (BLOCK, row_count))
    term = partial_softmax(
        fixed_queries,
        shard_rows[0].reshape(row_count, FIXED_HEADS, HEAD_DIM),
        shard_rows[1].reshape(row_count, FIXED_HEADS, HEAD_DIM),
        allowed,
    )
    fixed_state = merge_state(blank_state(FIXED_HEADS), term)
    column_own = (key_states[:, fixed_hi:], value_states[:, fixed_hi:], keep_flag)
    strided_queries = query_heads[:, LOCAL_HEADS + FIXED_HEADS :]
    shard_rows = (
        lax.all_gather(column_own[0], "grp", axis=0, tiled=True),
        lax.all_gather(column_own[1], "grp", axis=0, tiled=True),
        lax.all_gather(column_own[2], "grp", axis=0, tiled=True),
    )
    row_count = shard_rows[0].shape[0]
    row_window = jnp.arange(row_count, dtype=jnp.int32) // BLOCK
    usable = (row_window < window) & (shard_rows[2] > 0)
    allowed = jnp.broadcast_to(usable[None, :], (BLOCK, row_count))
    term = partial_softmax(
        strided_queries,
        shard_rows[0].reshape(row_count, STRIDED_HEADS, HEAD_DIM),
        shard_rows[1].reshape(row_count, STRIDED_HEADS, HEAD_DIM),
        allowed,
    )
    strided_state = merge_state(blank_state(STRIDED_HEADS), term)
    local_total = head_range(near_state, 0, LOCAL_HEADS)
    fixed_total = merge_state(
        head_range(near_state, LOCAL_HEADS, LOCAL_HEADS + FIXED_HEADS), fixed_state
    )
    strided_total = merge_state(
        head_range(near_state, LOCAL_HEADS + FIXED_HEADS, HEADS), strided_state
    )
    row_sum = jnp.concatenate([local_total[1], fixed_total[1], strided_total[1]], axis=0)
    weighted = jnp.concatenate([local_total[2], fixed_total[2], strided_total[2]], axis=0)
    result = weighted / row_sum[:, :, None]
    return jnp.transpose(result, (1, 0, 2)).reshape(BLOCK, HEADS * HEAD_DIM).astype(jnp.bfloat16)


def solution(mesh):
    return jax.shard_map(
        on_device,
        mesh=mesh,
        in_specs=(
            P(("grp", "seq"), None),
            P(("grp", "seq"), None),
            P(("grp", "seq"), None),
            P(("grp", "seq")),
            P(),
        ),
        out_specs=P(("grp", "seq"), None),
        check_vma=False,
    )
```

profile of v0, /device:TPU:1, one launch (start us, length us, event | category | flops | bytes accessed | tf_op | source)
XLA Modules:
  0.0 1218.3 jit_solution(5872520702400437514)
XLA Ops:
  7.4 2.3 copy.80
  9.7 1.6 copy.117
  11.3 0.7 dynamic_slice.3
  12.6 1.8 slice_select_fusion.1
  14.4 0.7 slice_select_fusion
  15.2 1.6 slice.52
  16.8 0.5 all-gather.11.cloned.1.call-update
  17.4 559.2 %all-reduce.3.cloned.1.call-done = (bf16[128,512]{0,1:T(8,128)(2,1)}, bf16[128,512]{0,1:T(8,128)(2,1)}) async-done(((bf16[128,512]{0,1:T(8,128)(2,1)}, bf16[128,512]{0,1:T(8,128)(2,1)}), (bf16[128,512]{0,1:T(8,128)(2,1)}, bf16[128,512]{0,1:T(8,128)(2,1)})) %all-reduce.3.cloned.1.call-update) | async-done | bytes 262160 | tf_op jit(solution)/shard_map/psum | solution.py:25
  576.7 2.1 collective-permute-start.2
  578.8 1.9 collective-permute-start.1
  580.7 1.9 collective-permute-start.5
  582.6 1.9 collective-permute-start.4
  584.6 1.9 collective-permute-start
  586.5 0.4 copy.75
  586.9 282.3 %psum.21 = bf16[128]{0:T(256)(128)(2,1)S(1)} all-reduce(bf16[128]{0:T(256)(128)(2,1)S(1)} %broadcast_select_fusion), channel_id=1, replica_groups=mesh['grp'=16,'seq'=32] {'seq'}, use_global_device_ids=true, to_apply=%region_4.5 | all-reduce | flops 128 | bytes 512 | tf_op jit(solution)/shard_map/psum | solution.py:25
  869.2 219.4 %all-gather = bf16[16,1,128]{2,1,0:T(2,128)(2,1)S(1)} all-gather(bf16[1,1,128]{2,1,0:T(2,128)(2,1)S(1)} %bitcast.74), channel_id=1, replica_groups=mesh['grp'=16,'seq'=32] {'grp'}, dimensions={0}, use_global_device_ids=true | all-gather | bytes 4352 | tf_op jit(solution)/shard_map/all_gather | solution.py:104
  1088.7 25.1 %all-gather.1 = bf16[16,1,128]{2,1,0:T(2,128)(2,1)S(1)} all-gather(bf16[1,1,128]{2,1,0:T(2,128)(2,1)S(1)} %get-tuple-element.36), channel_id=1, replica_groups=mesh['grp'=16,'seq'=32] {'grp'}, dimensions={0}, use_global_device_ids=true | all-gather | bytes 4352 | tf_op jit(solution)/shard_map/all_gather | solution.py:124
  1113.8 0.1 select_reduce_fusion
  1113.9 0.1 fusion.63
  1114.0 0.4 fusion.95
  1114.4 0.4 fusion.42
  1114.8 0.3 fusion.15
  1115.1 2.1 collective-permute-start.3
  1117.3 16.0 %collective-permute-done.3 = bf16[128]{0:T(256)(128)(2,1)S(1)} collective-permute-done((bf16[128]{0:T(256)(128)(2,1)S(1)}, bf16[128]{0:T(256)(128)(2,1)S(1)}, u32[]{:S(2)}, u32[]{:S(2)}) %collective-permute-start.3) | collective-permute-done | bytes 288 | tf_op jit(solution)/shard_map/ppermute | solution.py:20
  1133.3 1.5 copy.83
  1134.8 2.3 copy.88
  1137.1 1.6 fusion.96
  1138.7 0.3 fusion.19
  1139.0 1.6 fusion.94
  1140.6 0.3 fusion.17
  1141.0 0.5 fusion.40
  1141.4 0.7 copy-done.5
  1142.1 0.7 multiply_add_fusion
  1142.8 1.2 copy-done.1
  1144.0 3.9 copy.101
  1147.9 2.7 fusion.2
  1150.7 2.0 copy-done.3
  1152.6 1.2 fusion.3
  1153.8 2.9 bitcast_reduce_fusion
  1156.8 1.6 fusion.5
  1158.4 0.5 copy-done
  1159.0 0.4 copy-done.2
  1159.4 1.0 copy-done.6
  1160.4 1.7 fusion.55
  1162.1 43.3 %all-gather.9.cloned.1.call-done = bf16[2048,512]{0,1:T(8,128)(2,1)} async-done(((bf16[128,512]{0,1:T(8,128)(2,1)}), bf16[2048,512]{0,1:T(8,128)(2,1)}) %all-gather.9.cloned.1.call-update) | async-done | bytes 2097168 | tf_op jit(solution)/shard_map/all_gather | solution.py:103
  1205.4 4.0 fusion.56
  1209.4 0.2 fusion.14
  1209.6 1.2 copy.103
  (47 shorter events, 0.4 us)
Async XLA Ops:
  7.4 569.2 %all-reduce.3.cloned.1.call-start = ((), (), s32[]{:S(2)}) async-start(), calls=%async_computation.4 | async-start | bytes 524288 | tf_op jit(solution)/shard_map/psum | solution.py:25
  7.4 3.9 copy-start.9
  9.7 574.9 %copy-start.10 = (s32[128]{0:T(128)S(1)}, s32[128]{0:T(128)}, u32[]{:S(2)}) copy-start(s32[128]{0:T(128)} %param.8) | copy-start | bytes 1540
  9.7 576.9 %copy-start.7 = (bf16[128,3072]{1,0:T(8,128)(2,1)S(1)}, bf16[128,3072]{1,0:T(8,128)(2,1)}, u32[]{:S(2)}) copy-start(bf16[128,3072]{1,0:T(8,128)(2,1)} %param.5) | copy-start | bytes 2359300
  12.6 1101.4 %copy-start.8 = (bf16[128,3072]{1,0:T(8,128)(2,1)S(1)}, bf16[128,3072]{1,0:T(8,128)(2,1)}, u32[]{:S(2)}) copy-start(bf16[128,3072]{1,0:T(8,128)(2,1)} %param.6) | copy-start | bytes 2359300
  15.1 1128.9 %all-gather.13.cloned.1.call-start = ((), (), s32[]{:S(2)}) async-start(), calls=%async_computation.3 | async-start | bytes 2228224 | tf_op jit(solution)/shard_map/all_gather | solution.py:123
  16.7 1131.2 %all-gather.11.cloned.1.call-start = ((), (), s32[]{:S(2)}) async-start(), calls=%async_computation.2 | async-start | bytes 2228224 | tf_op jit(solution)/shard_map/all_gather | solution.py:122
  17.3 1136.5 %all-gather.7.cloned.1.call-start = ((), (), s32[]{:S(2)}) async-start(), calls=%async_computation | async-start | bytes 2228224 | tf_op jit(solution)/shard_map/all_gather | solution.py:102
  576.6 628.8 %all-gather.9.cloned.1.call-start = ((), (), s32[]{:S(2)}) async-start(), calls=%async_computation.1 | async-start | bytes 2228224 | tf_op jit(solution)/shard_map/all_gather | solution.py:103
  576.7 556.6 %collective-permute-start.2 = (bf16[128,3072]{1,0:T(8,128)(2,1)}, bf16[128,3072]{1,0:T(8,128)(2,1)}, u32[]{:S(2)}, u32[]{:S(2)}) collective-permute-start(bf16[128,3072]{1,0:T(8,128)(2,1)} %param.7), channel_id=1, source_target_pairs={{0,1},{1,2},{2,3},{3,4},{4,5},{5,6},{6,7},{7,8},{8,9},{9,10},{10,1... | collective-permute-start | bytes 2359304 | tf_op jit(solution)/shard_map/ppermute | solution.py:20
  578.8 560.2 %collective-permute-start.1 = (bf16[128,3072]{0,1:T(8,128)(2,1)}, bf16[128,3072]{0,1:T(8,128)(2,1)}, u32[]{:S(2)}, u32[]{:S(2)}) collective-permute-start(bf16[128,3072]{0,1:T(8,128)(2,1)} %copy.80), channel_id=1, source_target_pairs={{0,1},{1,2},{2,3},{3,4},{4,5},{5,6},{6,7},{7,8},{8,9},{9,10},{10,1... | collective-permute-start | bytes 2359304 | tf_op jit(solution)/shard_map/ppermute | solution.py:20
  580.7 554.1 %collective-permute-start.5 = (bf16[128,3072]{1,0:T(8,128)(2,1)}, bf16[128,3072]{1,0:T(8,128)(2,1)}, u32[]{:S(2)}, u32[]{:S(2)}) collective-permute-start(bf16[128,3072]{1,0:T(8,128)(2,1)} %param.7), channel_id=1, source_target_pairs={{0,2},{1,3},{2,4},{3,5},{4,6},{5,7},{6,8},{7,9},{8,10},{9,11},{10,... | collective-permute-start | bytes 2359304 | tf_op jit(solution)/shard_map/ppermute | solution.py:20
  582.6 554.4 %collective-permute-start.4 = (bf16[128,3072]{0,1:T(8,128)(2,1)}, bf16[128,3072]{0,1:T(8,128)(2,1)}, u32[]{:S(2)}, u32[]{:S(2)}) collective-permute-start(bf16[128,3072]{0,1:T(8,128)(2,1)} %copy.80), channel_id=1, source_target_pairs={{0,2},{1,3},{2,4},{3,5},{4,6},{5,7},{6,8},{7,9},{8,10},{9,11},{10,... | collective-permute-start | bytes 2359304 | tf_op jit(solution)/shard_map/ppermute | solution.py:20
  584.6 530.5 %collective-permute-start = (bf16[128]{0:T(256)(128)(2,1)S(1)}, bf16[128]{0:T(256)(128)(2,1)S(1)}, u32[]{:S(2)}, u32[]{:S(2)}) collective-permute-start(bf16[128]{0:T(256)(128)(2,1)S(1)} %get-tuple-element.37), channel_id=1, source_target_pairs={{0,1},{1,2},{2,3},{3,4},{4,5},{5,6},{6,7},{7,8},{8,9},{9,10},{10,1... | collective-permute-start | bytes 776 | tf_op jit(solution)/shard_map/ppermute | solution.py:20
  1115.1 18.1 %collective-permute-start.3 = (bf16[128]{0:T(256)(128)(2,1)S(1)}, bf16[128]{0:T(256)(128)(2,1)S(1)}, u32[]{:S(2)}, u32[]{:S(2)}) collective-permute-start(bf16[128]{0:T(256)(128)(2,1)S(1)} %get-tuple-element.37), channel_id=1, source_target_pairs={{0,2},{1,3},{2,4},{3,5},{4,6},{5,7},{6,8},{7,9},{8,10},{9,11},{10,... | collective-permute-start | bytes 776 | tf_op jit(solution)/shard_map/ppermute | solution.py:20
  1141.0 1.1 copy-start.5
  1142.8 1.2 copy-start.1
  1150.6 2.0 copy-start.3
  1153.8 5.1 copy-start.4
  1156.8 2.1 copy-start
  1156.8 2.6 copy-start.2
  1156.8 3.6 copy-start.6
  1205.4 4.0 slice-start
Sparse Core Ops, SparseCore 0:
  15.2 561.3 all-reduce.2
Sparse Core Ops, SparseCore 1:
  17.7 107.5 all-gather.12
  127.1 84.2 all-gather.10
  576.7 299.0 all-gather.6
  1133.3 72.0 all-gather.8
where the time goes:
time: 1220 us
  waiting for transfers between devices  619 us (51%)
  blocking collectives  527 us (43%)
  local copies, waits for them, and re-layouts  21.1 us (2%)
  matrix products  16.4 us (1%)
  between operations  16.2 us (1%)
    psum x1, waiting for transfers between devices, spread(): return lax.psum(kept, axis)  559 us
    psum x1, blocking collectives, spread(): return lax.psum(kept, axis)  282 us
    all_gather x1, blocking collectives, on_device(): lax.all_gather(summary_here[2], 'grp', axis=0, tiled=True)  219 us
    all_gather x1, waiting for transfers between devices, on_device(): lax.all_gather(summary_here[1], 'grp', axis=0, tiled=True)  43.3 us
    all_gather x1, blocking collectives, on_device(): lax.all_gather(column_own[2], 'grp', axis=0, tiled=True)  25.1 us
  transfers between devices with their start and end apart: 11, of which 3 were waited for; matrix products, arithmetic and copies ran while one was open for 2% of the time, Pallas kernels for 0%

commit v1 on v0

--- a/solution.py
+++ b/solution.py
@@ -121,7 +121,9 @@
     shard_rows = (
         lax.all_gather(column_own[0], "grp", axis=0, tiled=True),
         lax.all_gather(column_own[1], "grp", axis=0, tiled=True),
-        lax.all_gather(column_own[2], "grp", axis=0, tiled=True),
+        jnp.concatenate(
+            lax.all_to_all(jnp.stack([column_own[2]] * lax.axis_size("grp")), "grp", 0, 0), axis=0
+        ),
     )
     row_count = shard_rows[0].shape[0]
     row_window = jnp.arange(row_count, dtype=jnp.int32) // BLOCK

time: 1220 us -> 1190 us (0.975)
  blocking collectives: 527 us -> 472 us
  starting transfers between devices: 12.1 us -> 43.3 us
    all_gather x1, blocking collectives: 219 us -> 163 us  [on_device(): lax.all_gather(summary_here[2], 'grp', axis=0, tiled=True)]
    all_to_all x0 -> x1, starting transfers between devices: none -> 31.2 us  [on_device(): lax.all_to_all(jnp.stack([column_own[2]] * lax.axis_size('grp')), 'grp',...]
    psum x1, blocking collectives: 282 us -> 309 us  [spread(): return lax.psum(kept, axis)]
    all_gather x1 -> x0, blocking collectives: 25.1 us -> none  [on_device(): lax.all_gather(column_own[2], 'grp', axis=0, tiled=True)]
  transfers between devices with their start and end apart: 11 -> 12, of which waited for: 3 -> 3; matrix products, arithmetic and copies ran while one was open for 2% -> 2% of each run, Pallas kernels for 0% -> 0%
where the time goes in v1:
time: 1190 us
  waiting for transfers between devices  618 us (52%)
  blocking collectives  472 us (40%)
  starting transfers between devices  43.3 us (4%)
  local copies, waits for them, and re-layouts  21.6 us (2%)
  matrix products  16.5 us (1%)
  between operations  16 us (1%)
    psum x1, waiting for transfers between devices, spread(): return lax.psum(kept, axis)  559 us
    psum x1, blocking collectives, spread(): return lax.psum(kept, axis)  309 us
    all_gather x1, blocking collectives, on_device(): lax.all_gather(summary_here[2], 'grp', axis=0, tiled=True)  163 us
    all_gather x1, waiting for transfers between devices, on_device(): lax.all_gather(summary_here[1], 'grp', axis=0, tiled=True)  42 us
    all_to_all x1, starting transfers between devices, on_device(): lax.all_to_all(jnp.stack([column_own[2]] * lax.axis_size('grp')), 'grp',...  31.2 us
  transfers between devices with their start and end apart: 12, of which 3 were waited for; matrix products, arithmetic and copies ran while one was open for 2% of the time, Pallas kernels for 0%

profile of v1, /device:TPU:1, one launch (start us, length us, event | category | flops | bytes accessed | tf_op | source)
XLA Modules:
  0.0 1193.3 jit_solution(8748704284576065198)
XLA Ops:
  7.4 2.3 copy.108
  9.7 1.6 copy.145
  11.3 0.6 dynamic_slice.3
  12.4 1.7 slice_select_fusion.1
  14.1 0.7 slice_select_fusion
  14.8 1.6 slice.52
  16.5 0.5 all-gather.10.cloned.1.call-update
  17.1 559.2 %all-reduce.3.cloned.1.call-done = (bf16[128,512]{0,1:T(8,128)(2,1)}, bf16[128,512]{0,1:T(8,128)(2,1)}) async-done(((bf16[128,512]{0,1:T(8,128)(2,1)}, bf16[128,512]{0,1:T(8,128)(2,1)}), (bf16[128,512]{0,1:T(8,128)(2,1)}, bf16[128,512]{0,1:T(8,128)(2,1)})) %all-reduce.3.cloned.1.call-update) | async-done | bytes 262160 | tf_op jit(solution)/shard_map/psum | solution.py:25
  576.3 2.1 collective-permute-start.2
  578.4 1.9 collective-permute-start.1
  580.3 1.9 collective-permute-start.5
  582.3 1.9 collective-permute-start.4
  584.2 1.9 collective-permute-start
  586.2 0.6 stack.2
  586.8 31.2 %all-to-all-start = ((bf16[16,1,128]{2,1,0:T(2,128)(2,1)}), bf16[16,1,128]{2,1,0:T(2,128)(2,1)S(1)}, u32[]{:S(2)}, u32[]{:S(2)}) async-start(bf16[16,1,128]{2,1,0:T(2,128)(2,1)} %stack.2), calls=%async_computation | async-start | bytes 16384 | tf_op jit(solution)/shard_map/all_to_all | solution.py:125
  618.1 0.4 copy.103
  618.5 308.5 %psum.21 = bf16[128]{0:T(256)(128)(2,1)S(1)} all-reduce(bf16[128]{0:T(256)(128)(2,1)S(1)} %broadcast_select_fusion), channel_id=1, replica_groups=mesh['grp'=16,'seq'=32] {'seq'}, use_global_device_ids=true, to_apply=%region_4.5 | all-reduce | flops 128 | bytes 512 | tf_op jit(solution)/shard_map/psum | solution.py:25
  927.0 163.0 %all-gather = bf16[16,1,128]{2,1,0:T(2,128)(2,1)S(1)} all-gather(bf16[1,1,128]{2,1,0:T(2,128)(2,1)S(1)} %bitcast.72), channel_id=1, replica_groups=mesh['grp'=16,'seq'=32] {'grp'}, dimensions={0}, use_global_device_ids=true | all-gather | bytes 4352 | tf_op jit(solution)/shard_map/all_gather | solution.py:104
  1090.0 0.1 select_reduce_fusion
  1090.2 0.4 fusion.95
  1090.6 0.4 fusion.42
  1091.0 0.3 fusion.15
  1091.3 2.1 collective-permute-start.3
  1093.5 16.0 %collective-permute-done.3 = bf16[128]{0:T(256)(128)(2,1)S(1)} collective-permute-done((bf16[128]{0:T(256)(128)(2,1)S(1)}, bf16[128]{0:T(256)(128)(2,1)S(1)}, u32[]{:S(2)}, u32[]{:S(2)}) %collective-permute-start.3) | collective-permute-done | bytes 288 | tf_op jit(solution)/shard_map/ppermute | solution.py:20
  1109.5 1.5 copy.111
  1111.0 2.3 copy.116
  1113.3 1.6 fusion.96
  1114.9 0.3 fusion.19
  1115.2 1.6 fusion.94
  1116.8 0.3 fusion.17
  1117.2 0.5 fusion.40
  1117.7 0.7 copy-done.5
  1118.3 0.7 multiply_add_fusion
  1119.0 1.2 copy-done.1
  1120.2 3.9 copy.129
  1124.2 2.7 fusion.2
  1126.9 2.0 copy-done.3
  1128.8 1.2 fusion.3
  1130.1 2.9 bitcast_reduce_fusion
  1133.0 1.6 fusion.5
  1134.6 0.5 copy-done
  1135.2 0.4 copy-done.2
  1135.6 1.0 copy-done.6
  1136.6 1.7 fusion.55
  1138.3 42.0 %all-gather.8.cloned.1.call-done = bf16[2048,512]{0,1:T(8,128)(2,1)} async-done(((bf16[128,512]{0,1:T(8,128)(2,1)}), bf16[2048,512]{0,1:T(8,128)(2,1)}) %all-gather.8.cloned.1.call-update) | async-done | bytes 2097168 | tf_op jit(solution)/shard_map/all_gather | solution.py:103
  1180.4 4.0 fusion.56
  1184.3 0.2 fusion.14
  1184.5 1.2 copy.131
  (49 shorter events, 0.5 us)
Async XLA Ops:
  7.4 568.9 %all-reduce.3.cloned.1.call-start = ((), (), s32[]{:S(2)}) async-start(), calls=%async_computation.5 | async-start | bytes 524288 | tf_op jit(solution)/shard_map/psum | solution.py:25
  7.4 3.9 copy-start.9
  9.7 574.5 %copy-start.10 = (s32[128]{0:T(128)S(1)}, s32[128]{0:T(128)}, u32[]{:S(2)}) copy-start(s32[128]{0:T(128)} %param.8) | copy-start | bytes 1540
  9.7 608.4 %copy-start.7 = (bf16[128,3072]{1,0:T(8,128)(2,1)S(1)}, bf16[128,3072]{1,0:T(8,128)(2,1)}, u32[]{:S(2)}) copy-start(bf16[128,3072]{1,0:T(8,128)(2,1)} %param.5) | copy-start | bytes 2359300
  14.1 1076.1 %copy-start.8 = (bf16[128,3072]{1,0:T(8,128)(2,1)S(1)}, bf16[128,3072]{1,0:T(8,128)(2,1)}, u32[]{:S(2)}) copy-start(bf16[128,3072]{1,0:T(8,128)(2,1)} %param.6) | copy-start | bytes 2359300
  14.8 1105.4 %all-gather.12.cloned.1.call-start = ((), (), s32[]{:S(2)}) async-start(), calls=%async_computation.4 | async-start | bytes 2228224 | tf_op jit(solution)/shard_map/all_gather | solution.py:123
  16.4 1107.7 %all-gather.10.cloned.1.call-start = ((), (), s32[]{:S(2)}) async-start(), calls=%async_computation.3 | async-start | bytes 2228224 | tf_op jit(solution)/shard_map/all_gather | solution.py:122
  17.0 1113.0 %all-gather.6.cloned.1.call-start = ((), (), s32[]{:S(2)}) async-start(), calls=%async_computation.1 | async-start | bytes 2228224 | tf_op jit(solution)/shard_map/all_gather | solution.py:102
  576.3 533.2 %collective-permute-start.2 = (bf16[128,3072]{1,0:T(8,128)(2,1)}, bf16[128,3072]{1,0:T(8,128)(2,1)}, u32[]{:S(2)}, u32[]{:S(2)}) collective-permute-start(bf16[128,3072]{1,0:T(8,128)(2,1)} %param.7), channel_id=1, source_target_pairs={{0,1},{1,2},{2,3},{3,4},{4,5},{5,6},{6,7},{7,8},{8,9},{9,10},{10,1... | collective-permute-start | bytes 2359304 | tf_op jit(solution)/shard_map/ppermute | solution.py:20
  578.4 536.8 %collective-permute-start.1 = (bf16[128,3072]{0,1:T(8,128)(2,1)}, bf16[128,3072]{0,1:T(8,128)(2,1)}, u32[]{:S(2)}, u32[]{:S(2)}) collective-permute-start(bf16[128,3072]{0,1:T(8,128)(2,1)} %copy.108), channel_id=1, source_target_pairs={{0,1},{1,2},{2,3},{3,4},{4,5},{5,6},{6,7},{7,8},{8,9},{9,10},{10,1... | collective-permute-start | bytes 2359304 | tf_op jit(solution)/shard_map/ppermute | solution.py:20
  580.3 530.7 %collective-permute-start.5 = (bf16[128,3072]{1,0:T(8,128)(2,1)}, bf16[128,3072]{1,0:T(8,128)(2,1)}, u32[]{:S(2)}, u32[]{:S(2)}) collective-permute-start(bf16[128,3072]{1,0:T(8,128)(2,1)} %param.7), channel_id=1, source_target_pairs={{0,2},{1,3},{2,4},{3,5},{4,6},{5,7},{6,8},{7,9},{8,10},{9,11},{10,... | collective-permute-start | bytes 2359304 | tf_op jit(solution)/shard_map/ppermute | solution.py:20
  582.3 531.0 %collective-permute-start.4 = (bf16[128,3072]{0,1:T(8,128)(2,1)}, bf16[128,3072]{0,1:T(8,128)(2,1)}, u32[]{:S(2)}, u32[]{:S(2)}) collective-permute-start(bf16[128,3072]{0,1:T(8,128)(2,1)} %copy.108), channel_id=1, source_target_pairs={{0,2},{1,3},{2,4},{3,5},{4,6},{5,7},{6,8},{7,9},{8,10},{9,11},{10,... | collective-permute-start | bytes 2359304 | tf_op jit(solution)/shard_map/ppermute | solution.py:20
  584.2 507.1 %collective-permute-start = (bf16[128]{0:T(256)(128)(2,1)S(1)}, bf16[128]{0:T(256)(128)(2,1)S(1)}, u32[]{:S(2)}, u32[]{:S(2)}) collective-permute-start(bf16[128]{0:T(256)(128)(2,1)S(1)} %convert_element_type.33), channel_id=1, source_target_pairs={{0,1},{1,2},{2,3},{3,4},{4,5},{5,6},{6,7},{7,8},{8,9},{9,10},{10,1... | collective-permute-start | bytes 776 | tf_op jit(solution)/shard_map/ppermute | solution.py:20
  586.8 522.7 %all-to-all-start = ((bf16[16,1,128]{2,1,0:T(2,128)(2,1)}), bf16[16,1,128]{2,1,0:T(2,128)(2,1)S(1)}, u32[]{:S(2)}, u32[]{:S(2)}) async-start(bf16[16,1,128]{2,1,0:T(2,128)(2,1)} %stack.2), calls=%async_computation | async-start | bytes 16384 | tf_op jit(solution)/shard_map/all_to_all | solution.py:125
  618.0 562.4 %all-gather.8.cloned.1.call-start = ((), (), s32[]{:S(2)}) async-start(), calls=%async_computation.2 | async-start | bytes 2228224 | tf_op jit(solution)/shard_map/all_gather | solution.py:103
  1091.3 18.1 %collective-permute-start.3 = (bf16[128]{0:T(256)(128)(2,1)S(1)}, bf16[128]{0:T(256)(128)(2,1)S(1)}, u32[]{:S(2)}, u32[]{:S(2)}) collective-permute-start(bf16[128]{0:T(256)(128)(2,1)S(1)} %convert_element_type.33), channel_id=1, source_target_pairs={{0,2},{1,3},{2,4},{3,5},{4,6},{5,7},{6,8},{7,9},{8,10},{9,11},{10,... | collective-permute-start | bytes 776 | tf_op jit(solution)/shard_map/ppermute | solution.py:20
  1117.2 1.1 copy-start.5
  1119.0 1.2 copy-start.1
  1126.9 2.0 copy-start.3
  1130.0 5.1 copy-start.4
  1133.0 2.1 copy-start
  1133.0 2.6 copy-start.2
  1133.0 3.6 copy-start.6
  1180.4 4.0 slice-start
Sparse Core Ops, SparseCore 0:
  14.9 561.3 all-reduce.2
Sparse Core Ops, SparseCore 1:
  17.3 107.5 all-gather.11
  126.8 84.2 all-gather.9
  576.4 296.3 all-gather.5
  1109.6 70.7 all-gather.7
